TPU v7x, 512 devices: a whole 4x8x8 slice. The times are simulated.
512 devices in a mesh: stn: 16 (over x_lo, z), chan: 32 (over x_hi, y, core).
Axes of the slice: x: 4 (x_hi: 2, x_lo: 2; x = x_hi * 2 + x_lo), y: 8, z: 8, core: 2. Of those that a mesh axis runs over, the one named last changes fastest.
Arguments:
- positions: float32 [3, 256], P(None, 'stn'), may hold values from -1 to 1
- catalogue: float32 [7, 1024], P(None, 'chan'), may hold values from -1.5 to 1, as said below
- cluster_ids: int32 [16, 64], replicated, may hold values from 0 to 1023, as said below
- counts: int32 [16], replicated, may hold values from 16 to 64, as said below
- flag_mask: int32 [32, 256, 256], P('chan', 'stn'), may hold values 0 or 1
- thermal_noise: float32 [2, 4, 32, 256, 256], P(None, None, 'chan', 'stn'), may hold values from -3 to 3
- true_gains: float32 [2, 4, 16, 256], P(None, None, None, 'stn'), may hold values from -0.5 to 1.5, as said below
- start_gains: float32 [2, 4, 16, 256], P(None, None, None, 'stn'), may hold values from -0.5 to 1.2, as said below
Outputs:
- final_gains: float32 [2, 4, 16, 256], P(None, None, None, 'stn')
- residual: float32 [2, 4, 32, 256, 256], P(None, None, 'chan', 'stn')
Inputs may be any that keep to these rules, and one draw needn't show every extreme that they name: `catalogue`: rows: direction cosines l and m within -0.4 to 0.4, Stokes I from 0.02 to 1, Stokes Q, U and V each at most 0.3 I in size, spectral index from -1.5 to -0.5. `cluster_ids`: each of the 1024 catalogue entries appears exactly once. Direction d uses the first counts[d] slots of its row of cluster_ids; some direction uses all 64. `true_gains`: real parts of the diagonal entries lie in 0.5 to 1.5; every other entry lies in -0.5 to 0.5. `start_gains`: real parts of the diagonal entries lie in 0.8 to 1.2; every other entry lies in -0.5 to 0.5.
All inputs are finite; a program needn't handle non-finite values. No bound on the sum of `flag_mask` on one device may be relied on, other than what follows from the above.
Results may differ from a plain program's by a relative error of at most 0.0003.
Values sent between devices are 32-bit elements; how exact they have to be, the bound alone decides.
A program may use at most 128 MiB of HBM per device.

v0:
```python
import math

import jax
import jax.numpy as jnp
from jax import lax
from jax.sharding import PartitionSpec as P

ITERS = 3


band_spread = 6.0
ridge_term = 1.0
phase_scale = 2.0 * math.pi * 20.0


def complex_mul(left_real, left_imag, right_real, right_imag):
    return (
        left_real * right_real - left_imag * right_imag,
        left_real * right_imag + left_imag * right_real,
    )


def jones_mul(left, right):
    reals = []
    imags = []
    for out_row in range(2):
        for out_col in range(2):
            first_real, first_imag = complex_mul(
                left[0, 2 * out_row], left[1, 2 * out_row], right[0, out_col], right[1, out_col]
            )
            second_real, second_imag = complex_mul(
                left[0, 2 * out_row + 1],
                left[1, 2 * out_row + 1],
                right[0, 2 + out_col],
                right[1, 2 + out_col],
            )
            reals.append(first_real + second_real)
            imags.append(first_imag + second_imag)
    return jnp.stack([jnp.stack(reals), jnp.stack(imags)])


def jones_mul_adj(left, right):
    reals = []
    imags = []
    for out_row in range(2):
        for out_col in range(2):
            first_real, first_imag = complex_mul(
                left[0, 2 * out_row],
                left[1, 2 * out_row],
                right[0, 2 * out_col],
                -right[1, 2 * out_col],
            )
            second_real, second_imag = complex_mul(
                left[0, 2 * out_row + 1],
                left[1, 2 * out_row + 1],
                right[0, 2 * out_col + 1],
                -right[1, 2 * out_col + 1],
            )
            reals.append(first_real + second_real)
            imags.append(first_imag + second_imag)
    return jnp.stack([jnp.stack(reals), jnp.stack(imags)])


def sky_terms(catalogue, cluster_ids, counts):
    chosen = jnp.take(catalogue, cluster_ids, axis=1)
    slots = lax.broadcasted_iota(jnp.int32, cluster_ids.shape, 1)
    active = (slots < counts[:, None]).astype(jnp.float32)
    return (chosen, active)


def station_phase(station_pos, chosen, frequencies):
    depth = jnp.sqrt(1.0 - chosen[0] * chosen[0] - chosen[1] * chosen[1]) - 1.0
    geometry = (
        station_pos[0][None, :, None] * chosen[0][:, None, :]
        + station_pos[1][None, :, None] * chosen[1][:, None, :]
        + station_pos[2][None, :, None] * depth[:, None, :]
    )
    return phase_scale * frequencies[:, None, None, None] * geometry[None]


def brightness(chosen, active, frequencies):
    scaled = frequencies[:, None, None] ** chosen[6][None] * active[None]
    real_part = jnp.stack(
        [
            scaled * (chosen[2] + chosen[3]),
            scaled * chosen[4],
            scaled * chosen[4],
            scaled * (chosen[2] - chosen[3]),
        ]
    )
    zero_fill = jnp.zeros_like(scaled)
    imag_part = jnp.stack([zero_fill, scaled * chosen[5], -scaled * chosen[5], zero_fill])
    return (real_part, imag_part)


def near_products(phase_near, bright_real, bright_imag):
    cosine_near = jnp.cos(phase_near)[None]
    sine_near = jnp.sin(phase_near)[None]
    real_side = bright_real[:, :, :, None, :]
    imag_side = bright_imag[:, :, :, None, :]
    return (
        cosine_near * real_side - sine_near * imag_side,
        cosine_near * imag_side + sine_near * real_side,
    )


def contract(left, right):
    return jnp.einsum("xcdpk,cdqk->xcdqp", left, right, precision=lax.Precision.HIGHEST)


def far_contract(wide_real, wide_imag, phase_far):
    cosine_far = jnp.cos(phase_far)
    sine_far = jnp.sin(phase_far)
    real_part = contract(wide_real, cosine_far) + contract(wide_imag, sine_far)
    imag_part = contract(wide_imag, cosine_far) - contract(wide_real, sine_far)
    return jnp.stack([real_part, imag_part])


def gain_update(current, numerator, normal):
    upper_diag = normal[0, 0] + ridge_term
    lower_diag = normal[0, 3] + ridge_term
    cross_real = normal[0, 1]
    cross_imag = normal[1, 1]
    determinant = upper_diag * lower_diag - cross_real * cross_real - cross_imag * cross_imag
    zero_fill = jnp.zeros_like(upper_diag)
    inverse = (
        jnp.stack(
            [
                jnp.stack([lower_diag, -cross_real, -cross_real, upper_diag]),
                jnp.stack([zero_fill, -cross_imag, cross_imag, zero_fill]),
            ]
        )
        / determinant
    )
    return 0.5 * (current + jones_mul(numerator, inverse))


def visit_groups(payload, block_terms, initial):
    return block_terms(initial, lax.all_gather(payload, "stn", axis=1, tiled=True), jnp.int32(0))


def on_device(
    positions, catalogue, cluster_ids, counts, flag_mask, thermal_noise, true_gains, start_gains
):
    every_entry = lax.all_gather(catalogue, "chan", axis=1, tiled=True)
    chosen, active = sky_terms(every_entry, cluster_ids, counts)
    chan_count = thermal_noise.shape[2]
    group_size = true_gains.shape[3]
    directions = true_gains.shape[2]
    cycle_size = lax.axis_size("stn")
    total_stations = group_size * cycle_size
    channels = lax.axis_index("chan") * chan_count + jnp.arange(chan_count, dtype=jnp.int32)
    frequencies = 1.0 + band_spread * channels.astype(jnp.float32) / (
        chan_count * lax.axis_size("chan")
    )
    group_index = lax.axis_index("stn")
    near_index = group_index * group_size + jnp.arange(group_size, dtype=jnp.int32)
    bright_real, bright_imag = brightness(chosen, active, frequencies)
    wide_real, wide_imag = near_products(
        station_phase(positions, chosen, frequencies), bright_real, bright_imag
    )

    def model_terms(totals, portion, offset):
        members = portion.shape[1]
        far_true = portion[3:].reshape(2, 4, directions, members)
        coherent = far_contract(
            wide_real, wide_imag, station_phase(portion[0:3], chosen, frequencies)
        )
        noise_block = jnp.swapaxes(thermal_noise, 3, 4)
        true_part = jones_mul(
            true_gains[:, :, None, :, None, :],
            jones_mul_adj(coherent, far_true[:, :, None, :, :, None]),
        )
        observed = noise_block + true_part.sum(axis=3)
        return (coherent, observed)

    model_payload = jnp.concatenate(
        [positions, true_gains.reshape(8 * directions, group_size)], axis=0
    )
    model_initial = (
        jnp.zeros((2, 4, chan_count, directions, total_stations, group_size), jnp.float32),
        jnp.zeros((2, 4, chan_count, total_stations, group_size), jnp.float32),
    )
    coherency_all, observed_all = visit_groups(model_payload, model_terms, model_initial)
    current = start_gains
    residual = jnp.zeros((2, 4, chan_count, group_size, total_stations), jnp.float32)
    for iteration in range(ITERS):

        def block_terms(totals, portion, offset):
            members = portion.shape[1]
            far_current = portion.reshape(2, 4, directions, members)
            far_index = jnp.arange(members, dtype=jnp.int32)
            flag_block = jnp.swapaxes(flag_mask, 1, 2)
            weight = flag_block.astype(jnp.float32) * (
                far_index[:, None] != near_index[None, :]
            ).astype(jnp.float32)
            product = jones_mul_adj(coherency_all, far_current[:, :, None, :, :, None])
            predicted = jones_mul(current[:, :, None, :, None, :], product).sum(axis=3)
            misfit = weight * (observed_all - predicted)
            cross_sum = jones_mul_adj(misfit[:, :, :, None], product).sum(axis=(2, 4))
            normal = (weight[:, None] * jones_mul_adj(product, product)).sum(axis=(2, 4))
            residual = jnp.swapaxes(misfit, 3, 4)
            return (cross_sum, normal, residual)

        zero_terms = jnp.zeros_like(current)
        initial = (
            zero_terms,
            zero_terms,
            jnp.zeros((2, 4, chan_count, group_size, total_stations), jnp.float32),
        )
        cross_sum, normal, residual = visit_groups(
            current.reshape(8 * directions, group_size), block_terms, initial
        )
        solve_cross_sum = cross_sum
        solve_normal = normal
        solve_cross_sum, solve_normal = lax.psum((solve_cross_sum, solve_normal), "chan")
        current = gain_update(
            current, solve_cross_sum + jones_mul(current, solve_normal), solve_normal
        )
    return (current, residual)


def solution(mesh):
    return jax.shard_map(
        on_device,
        mesh=mesh,
        in_specs=(
            P(None, "stn"),
            P(None, "chan"),
            P(),
            P(),
            P("chan", "stn", None),
            P(None, None, "chan", "stn", None),
            P(None, None, None, "stn"),
            P(None, None, None, "stn"),
        ),
        out_specs=(P(None, None, None, "stn"), P(None, None, "chan", "stn", None)),
        check_vma=False,
    )
```

profile of v0, /device:TPU:64, one launch (start us, length us, event | category | flops | bytes accessed | tf_op | source)
XLA Modules:
  0.0 615.4 jit_solution(8883503476050904897)
XLA Ops:
  0.7 0.8 slice_bitcast_fusion.118
  1.5 0.7 compare_and_fusion
  2.2 0.9 copy.633
  3.1 0.9 copy.632
  4.0 0.8 copy.477
  4.8 0.7 compare_select_fusion
  5.6 0.8 fusion.319
  6.4 0.8 slice_bitcast_fusion.102
  7.2 0.8 slice_bitcast_fusion.112
  8.0 36.2 %all_gather.17 = f32[128,256]{0,1:T(8,128)S(1)} all-gather(f32[128,16]{0,1:T(8,128)S(1)} %copy.633), channel_id=1, replica_groups=mesh['stn'=16,'chan'=32] {'stn'}, dimensions={1}, use_global_device_ids=true | all-gather | bytes 139264 | tf_op jit(solution)/shard_map/all_gather | solution.py:139
  44.4 42.4 %all-gather = f32[32,32,7]{1,2,0:T(8,128)S(1)} all-gather(f32[1,32,7]{1,2,0:T(8,128)S(1)} %bitcast.2350), channel_id=1, replica_groups=mesh['stn'=16,'chan'=32] {'chan'}, dimensions={0}, use_global_device_ids=true | all-gather | bytes 29568 | tf_op jit(solution)/shard_map/all_gather | solution.py:145
  86.7 34.5 %all_gather.15 = f32[131,256]{0,1:T(8,128)S(1)} all-gather(f32[131,16]{0,1:T(8,128)S(1)} %pad_maximum_fusion.10), channel_id=1, replica_groups=mesh['stn'=16,'chan'=32] {'stn'}, dimensions={1}, use_global_device_ids=true | all-gather | bytes 142528 | tf_op jit(solution)/shard_map/all_gather | solution.py:139
  122.0 2.8 gather_fusion
  125.8 4.8 fusion.6
  130.6 4.8 fusion.4
  135.5 5.0 fusion.9
  140.6 4.8 fusion.3
  151.3 0.7 copy-done.1
  153.7 128.6 %all-reduce.2 = (f32[2,4,16,16]{3,2,1,0:T(8,128)S(1)}, f32[2,4,16,16]{3,2,1,0:T(8,128)S(1)}) all-reduce(f32[2,4,16,16]{3,2,1,0:T(8,128)S(1)} %maximum_reduce_fusion.2, f32[2,4,16,16]{3,2,1,0:T(8,128)S(1)} %fusion), channel_id=1, replica_groups=mesh['stn'=16,'chan'=32] {'chan'}, use_global_device_ids=true, to_apply=%region_3.4 | all-reduce | flops 4096 | bytes 32768 | tf_op jit(solution)/shard_map/psum | solution.py:216
  282.7 30.4 %all_gather.18 = f32[128,256]{0,1:T(8,128)S(1)} all-gather(f32[128,16]{0,1:T(8,128)S(1)} %copy.634), channel_id=1, replica_groups=mesh['stn'=16,'chan'=32] {'stn'}, dimensions={1}, use_global_device_ids=true | all-gather | bytes 139264 | tf_op jit(solution)/shard_map/all_gather | solution.py:139
  318.0 128.6 %all-reduce.1 = (f32[2,4,16,16]{3,2,1,0:T(8,128)S(1)}, f32[2,4,16,16]{3,2,1,0:T(8,128)S(1)}) all-reduce(f32[2,4,16,16]{3,2,1,0:T(8,128)S(1)} %maximum_reduce_fusion.4, f32[2,4,16,16]{3,2,1,0:T(8,128)S(1)} %fusion.1), channel_id=1, replica_groups=mesh['stn'=16,'chan'=32] {'chan'}, use_global_device_ids=true, to_apply=%region_8.9 | all-reduce | flops 4096 | bytes 32768 | tf_op jit(solution)/shard_map/psum | solution.py:216
  447.0 32.3 %all_gather.19 = f32[128,256]{0,1:T(8,128)S(1)} all-gather(f32[128,16]{0,1:T(8,128)S(1)} %copy.635), channel_id=1, replica_groups=mesh['stn'=16,'chan'=32] {'stn'}, dimensions={1}, use_global_device_ids=true | all-gather | bytes 139264 | tf_op jit(solution)/shard_map/all_gather | solution.py:139
  482.5 0.7 fusion.285
  485.4 128.6 %all-reduce = (f32[2,4,16,16]{3,2,1,0:T(8,128)S(1)}, f32[2,4,16,16]{3,2,1,0:T(8,128)S(1)}) all-reduce(f32[2,4,16,16]{3,2,1,0:T(8,128)S(1)} %maximum_reduce_fusion.6, f32[2,4,16,16]{3,2,1,0:T(8,128)S(1)} %fusion.2), channel_id=1, replica_groups=mesh['stn'=16,'chan'=32] {'chan'}, use_global_device_ids=true, to_apply=%region_13.14 | all-reduce | flops 4096 | bytes 32768 | tf_op jit(solution)/shard_map/psum | solution.py:216
  (183 shorter events, 20.9 us)
Async XLA Ops:
  0.6 43.7 %copy-start.2 = (f32[7,32]{1,0:T(8,128)S(1)}, f32[7,32]{1,0:T(8,128)}, u32[]{:S(2)}) copy-start(f32[7,32]{1,0:T(8,128)} %param.9) | copy-start | bytes 2692
  121.7 3.4 copy-start.3
  151.0 0.9 copy-start.1
  153.3 128.9 %copy-start = (f32[2,4,16,16]{3,2,1,0:T(8,128)S(1)}, f32[2,4,16,16]{3,2,1,0:T(8,128)}, u32[]{:S(2)}) copy-start(f32[2,4,16,16]{3,2,1,0:T(8,128)} %param.15) | copy-start | bytes 24580
where the time goes:
time: 625 us; the launch traced here: 615 us
  blocking collectives  561 us (90%)
  other arithmetic  22.3 us (4%)
  matrix products  19.4 us (3%)
  local copies, waits for them, and re-layouts  9.99 us (2%)
    psum x3, blocking collectives, on_device(): lax.psum((solve_cross_sum, solve_normal), 'chan')  386 us
    all_gather x4, blocking collectives, visit_groups(): lax.all_gather(payload, 'stn', axis=1, tiled=True)  133 us
    all_gather x1, blocking collectives, on_device(): every_entry = lax.all_gather(catalogue, 'chan', axis=1, tiled=True)  42.4 us
    dot_general x4, matrix products, contract(): jnp.einsum('xcdpk,cdqk->xcdqp', left, right, precision=lax.Precision.HIGH...  19.4 us

commit v1 on v0

v1 whole, which is shorter than its diff:
```python
import math

import jax
import jax.numpy as jnp
from jax import lax
from jax.experimental import pallas as pl
from jax.experimental.pallas import tpu as pltpu
from jax.sharding import PartitionSpec as P

ITERS = 3
LANES = 128
MESH = pl.DeviceIdType.MESH

band_spread = 6.0
ridge_term = 1.0
turn_scale = 20.0

SINE = (3.1415926401307073, -5.167710083507893, 2.5500775232145596, -0.5982912856201866, 0.07765766030500078)
COSINE = (
    0.9999999997799042,
    -4.9348021370788056,
    4.0587091595557485,
    -1.3352120030440895,
    0.23493731378565055,
    -0.024396324298134327,
)


def horner(terms, square):
    value = square * terms[-1] + terms[-2]
    for term in terms[-3::-1]:
        value = value * square + term
    return value


def turn_wave(turns):
    rest = turns - jnp.floor(turns + 0.5)
    square = rest * rest
    half_sine = rest * horner(SINE, square)
    half_cosine = horner(COSINE, square)
    twice = half_sine + half_sine
    return 1.0 - twice * half_sine, twice * half_cosine


def split_pair(value):
    high = value.astype(jnp.bfloat16)
    return high, (value - high.astype(jnp.float32)).astype(jnp.bfloat16)


def cmul(a, b):
    return a[0] * b[0] - a[1] * b[1], a[0] * b[1] + a[1] * b[0]


def cmul_conj(a, b):
    return a[0] * b[0] + a[1] * b[1], a[1] * b[0] - a[0] * b[1]


def cadd(a, b):
    return a[0] + b[0], a[1] + b[1]


def mat_mul(left, right):
    return [
        cadd(cmul(left[2 * i], right[j]), cmul(left[2 * i + 1], right[2 + j]))
        for i in range(2)
        for j in range(2)
    ]


def mat_mul_adj(left, right):
    return [
        cadd(cmul_conj(left[2 * i], right[2 * j]), cmul_conj(left[2 * i + 1], right[2 * j + 1]))
        for i in range(2)
        for j in range(2)
    ]


def start_copy(src, dst, send_sem, recv_sem, peer):
    copy = pltpu.make_async_remote_copy(
        src_ref=src,
        dst_ref=dst,
        send_sem=send_sem,
        recv_sem=recv_sem,
        device_id=peer,
        device_id_type=MESH,
    )
    copy.start()
    return copy


def kernel(
    sizes,
    positions,
    catalogue,
    ids,
    counts,
    flags,
    noise,
    true_gains,
    start_gains,
    final,
    residual,
    square,
    onehot,
    own_cat,
    every_cat,
    parts_cat,
    own_place,
    every_place,
    place_rows,
    own_gains,
    every_gains,
    true_far,
    gain_far,
    near_true,
    near_gain,
    coherent,
    product,
    observed,
    predicted,
    weight,
    misfit,
    cross_sum,
    normal,
    pair,
    mine,
    sums,
    fresh,
    spread,
    cat_send,
    cat_recv,
    place_send,
    place_recv,
    gain_send,
    gain_recv,
    pair_send,
    pair_recv,
    sum_send,
    sum_recv,
    fresh_send,
    fresh_recv,
    turn_send,
    turn_recv,
):
    groups, chans, dirs, slots, members, chan_total = sizes
    chips = chans // 2
    group = lax.axis_index("stn")
    channel = lax.axis_index("chan")
    chip = channel // 2
    core = lax.rem(channel, 2)
    stations = groups * members
    entries = chans * catalogue.shape[1]
    half = members // 2

    chan_peers = [{"chan": lax.rem(channel + step, chans)} for step in range(1, chans)]
    stn_peers = [{"stn": lax.rem(group + step, groups)} for step in range(1, groups)]
    sibling = {"chan": chip * 2 + 1 - core}
    chip_peers = [{"chan": lax.rem(chip + step, chips) * 2 + core} for step in range(1, chips)]
    cross_peers = [
        {"stn": lax.rem(group + step, groups), "chan": chip * 2 + 1 - core}
        for step in range(1, groups)
    ]

    barrier = pltpu.get_barrier_semaphore()
    greeted = chan_peers + stn_peers + cross_peers
    for peer in greeted:
        pl.semaphore_signal(barrier, inc=1, device_id=peer, device_id_type=MESH)

    square[...] = jnp.zeros_like(square)
    for copy_at in range(3):
        square[32 * copy_at : 32 * copy_at + 7, 0 : catalogue.shape[1]] = catalogue[...]
    own_cat[...] = jnp.transpose(square[...])[0 : catalogue.shape[1], :]
    square[...] = jnp.zeros_like(square)
    square[:, 0:members] = true_gains[...]
    own_gains[:, 0:LANES] = jnp.transpose(square[...])[0:members, :]
    square[:, 0:members] = start_gains[...]
    own_gains[:, LANES : 2 * LANES] = jnp.transpose(square[...])[0:members, :]
    own_place[...] = jnp.zeros_like(own_place)
    own_place[0:3, 0:members] = positions[...]

    pl.semaphore_wait(barrier, len(greeted))

    cat_copies = [
        start_copy(own_cat, every_cat.at[channel], cat_send.at[i], cat_recv.at[i], peer)
        for i, peer in enumerate(chan_peers)
    ]
    place_copies = [
        start_copy(own_place, every_place.at[group], place_send.at[i], place_recv.at[i], peer)
        for i, peer in enumerate(stn_peers)
    ]
    gain_copies = [
        start_copy(own_gains, every_gains.at[group], gain_send.at[i], gain_recv.at[i], peer)
        for i, peer in enumerate(stn_peers)
    ]
    every_cat[channel] = own_cat[...]
    every_place[group] = own_place[...]
    every_gains[group] = own_gains[...]
    near_true[...] = own_gains[:, 0:LANES]
    near_gain[...] = own_gains[:, LANES : 2 * LANES]

    near_index = group * members + lax.broadcasted_iota(jnp.int32, (members, stations), 0)
    far_index = lax.broadcasted_iota(jnp.int32, (members, stations), 1)
    weight[...] = jnp.where(near_index != far_index, flags[...].astype(jnp.float32), 0.0)

    square[...] = jnp.zeros_like(square)
    square[0:dirs, 0:slots] = ids[...].astype(jnp.float32)
    ids_turned = jnp.transpose(square[...])[0:slots, :]
    square[0:slots, :] = ids_turned
    lane_column = lax.broadcasted_iota(jnp.int32, (slots, LANES), 1)
    entry_at = lax.broadcasted_iota(jnp.int32, (slots, entries), 1).astype(jnp.float32)

    def mark(direction, carry):
        named = jnp.sum(
            jnp.where(lane_column == direction, square[0:slots, :], 0.0), axis=1, keepdims=True
        )
        onehot[direction] = jnp.where(named == entry_at, 1.0, 0.0).astype(jnp.bfloat16)
        return carry

    lax.fori_loop(0, dirs, mark, 0)

    frequency = 1.0 + band_spread * channel.astype(jnp.float32) / chan_total
    log_frequency = jnp.log(jnp.full((1, LANES), frequency, jnp.float32))
    lane_row = lax.broadcasted_iota(jnp.int32, (1, LANES), 1)
    imag_lane = lane_row >= 4 * members
    entry_lane = lax.rem(lane_row // members, 4)

    for copy in cat_copies:
        copy.wait_recv()
    whole = every_cat[...].reshape(entries, LANES)
    first = whole.astype(jnp.bfloat16).astype(jnp.float32)
    second = (whole - first).astype(jnp.bfloat16).astype(jnp.float32)
    third = whole - first - second
    wide_lane = lax.broadcasted_iota(jnp.int32, (entries, LANES), 1)
    parts_cat[...] = jnp.where(
        wide_lane < 32, first, jnp.where(wide_lane < 64, second, third)
    ).astype(jnp.bfloat16)

    for copy in place_copies:
        copy.wait_recv()
    per_row = LANES // members
    scale = turn_scale * frequency
    for block in range(groups // per_row):
        joined = every_place[block * per_row]
        for at in range(1, per_row):
            joined = joined + pltpu.roll(every_place[block * per_row + at], members * at, 1)
        place_rows[:, block * LANES : (block + 1) * LANES] = joined * scale
    tiled = own_place[...] * scale
    for shift in (members, 2 * members, 4 * members):
        tiled = tiled + pltpu.roll(tiled, shift, 1)

    def model(direction, carry):
        picked = lax.dot_general(
            onehot[direction],
            parts_cat[...],
            (((1,), (0,)), ((), ())),
            preferred_element_type=jnp.float32,
        )
        picked = picked + pltpu.roll(picked, LANES - 32, 1) + pltpu.roll(picked, LANES - 64, 1)

        def column(at):
            return jnp.broadcast_to(picked[:, at : at + 1], (slots, LANES))

        cos_l, cos_m = column(0), column(1)
        depth = jnp.sqrt(1.0 - cos_l * cos_l - cos_m * cos_m) - 1.0
        rows = lax.broadcasted_iota(jnp.int32, (slots, LANES), 0)
        scaled = jnp.where(
            rows < counts[direction], jnp.exp(column(6) * log_frequency), 0.0
        )
        stokes_i, stokes_q, stokes_u, stokes_v = (scaled * column(at) for at in (2, 3, 4, 5))
        bright_real = jnp.where(
            entry_lane == 0,
            stokes_i + stokes_q,
            jnp.where(entry_lane == 3, stokes_i - stokes_q, stokes_u),
        )
        bright_imag = jnp.where(
            entry_lane == 1, stokes_v, jnp.where(entry_lane == 2, -stokes_v, 0.0)
        )
        near_cos, near_sin = turn_wave(
            tiled[0:1, :] * cos_l + tiled[1:2, :] * cos_m + tiled[2:3, :] * depth
        )
        real_side = jnp.where(imag_lane, bright_imag, bright_real)
        imag_side = jnp.where(imag_lane, bright_real, -bright_imag)
        upper = real_side * near_cos + imag_side * near_sin
        lower = real_side * near_sin - imag_side * near_cos
        near_side = jnp.transpose(jnp.concatenate([upper, lower], axis=0))
        near_high, near_low = split_pair(near_side)
        blocks = []
        for block in range(stations // LANES):
            lanes = slice(block * LANES, (block + 1) * LANES)
            blocks.append(
                jnp.concatenate(
                    turn_wave(
                        place_rows[0:1, lanes] * cos_l
                        + place_rows[1:2, lanes] * cos_m
                        + place_rows[2:3, lanes] * depth
                    ),
                    axis=0,
                )
            )
        far_high, far_low = split_pair(jnp.concatenate(blocks, axis=1))

        def times(left, right):
            return jnp.dot(left, right, preferred_element_type=jnp.float32)

        result = times(near_high, far_high) + (
            times(near_low, far_high) + times(near_high, far_low)
        )
        coherent[direction] = result.reshape(8, members, stations)
        return carry

    lax.fori_loop(0, dirs, model, 0)

    for copy in gain_copies:
        copy.wait_recv()
    turned = jnp.transpose(every_gains[:, :, 0:LANES].reshape(stations, LANES))
    true_far[...] = turned
    turned = jnp.transpose(every_gains[:, :, LANES : 2 * LANES].reshape(stations, LANES))
    gain_far[...] = turned

    near_lane = lax.broadcasted_iota(jnp.int32, (members, LANES), 1)
    halves = [slice(at * LANES, (at + 1) * LANES) for at in range(stations // LANES)]

    def near_matrix(ref, direction):
        whole_near = ref[...]
        return [
            tuple(
                jnp.sum(
                    jnp.where(near_lane == (part * 4 + entry) * dirs + direction, whole_near, 0.0),
                    axis=1,
                    keepdims=True,
                )
                for part in range(2)
            )
            for entry in range(4)
        ]

    def far_matrix(ref, direction, lanes):
        return [
            tuple(
                ref[pl.ds((part * 4 + entry) * dirs + direction, 1), :][:, lanes]
                for part in range(2)
            )
            for entry in range(4)
        ]

    def planes(ref, lanes, *lead):
        return [
            tuple(ref[(*lead, part * 4 + entry, slice(None), lanes)] for part in range(2))
            for entry in range(4)
        ]

    def add_planes(ref, lanes, matrix):
        for entry in range(4):
            for part in range(2):
                ref[part * 4 + entry, :, lanes] += matrix[entry][part]

    observed[...] = noise[...]

    def observe(direction, carry):
        near = near_matrix(near_true, direction)
        for lanes in halves:
            spun = mat_mul_adj(
                planes(coherent, lanes, direction), far_matrix(true_far, direction, lanes)
            )
            add_planes(observed, lanes, mat_mul(near, spun))
        return carry

    lax.fori_loop(0, dirs, observe, 0)

    def predict(direction, carry):
        near = near_matrix(near_gain, direction)
        totals = [0.0] * 4
        for lanes in halves:
            spun = mat_mul_adj(
                planes(coherent, lanes, direction), far_matrix(gain_far, direction, lanes)
            )
            add_planes(predicted, lanes, mat_mul(near, spun))
            for entry in range(4):
                for part in range(2):
                    product[direction, part * 4 + entry, :, lanes] = spun[entry][part]
            weighted = [
                tuple(weight[:, lanes] * value for value in spun[entry]) for entry in range(2)
            ]
            first_power = sum(
                weighted[entry][part] * spun[entry][part]
                for entry in range(2)
                for part in range(2)
            )
            second_power = weight[:, lanes] * sum(
                spun[entry][part] * spun[entry][part] for entry in (2, 3) for part in range(2)
            )
            cross = cadd(cmul_conj(weighted[0], spun[2]), cmul_conj(weighted[1], spun[3]))
            for at, value in enumerate((first_power, second_power, *cross)):
                totals[at] = totals[at] + value
        collected = normal[...]
        for at in range(4):
            collected = jnp.where(
                near_lane == at * dirs + direction,
                jnp.sum(totals[at], axis=1, keepdims=True),
                collected,
            )
        normal[...] = collected
        return carry

    def correlate(direction, carry):
        totals = [[0.0, 0.0] for entry in range(4)]
        for lanes in halves:
            found = mat_mul_adj(planes(misfit, lanes), planes(product, lanes, direction))
            for entry in range(4):
                for part in range(2):
                    totals[entry][part] = totals[entry][part] + found[entry][part]
        collected = cross_sum[...]
        for entry in range(4):
            for part in range(2):
                collected = jnp.where(
                    near_lane == (part * 4 + entry) * dirs + direction,
                    jnp.sum(totals[entry][part], axis=1, keepdims=True),
                    collected,
                )
        cross_sum[...] = collected
        return carry

    pending = cat_copies + place_copies + gain_copies
    kept = pl.ds(pl.multiple_of(core * half, half), half)
    away = pl.ds(pl.multiple_of((1 - core) * half, half), half)
    cross_sum[...] = jnp.zeros_like(cross_sum)
    normal[...] = jnp.zeros_like(normal)

    for iteration in range(ITERS):
        predicted[...] = jnp.zeros_like(predicted)
        lax.fori_loop(0, dirs, predict, 0)
        for plane in range(8):
            misfit[plane] = weight[...] * (observed[plane] - predicted[plane])
        lax.fori_loop(0, dirs, correlate, 0)
        mine[iteration, :, 0:LANES] = cross_sum[...]
        mine[iteration, :, LANES : 2 * LANES] = normal[...]

        swap = start_copy(
            mine.at[iteration, away],
            pair.at[iteration],
            pair_send.at[iteration],
            pair_recv.at[iteration],
            sibling,
        )
        swap.wait_recv()
        pending.append(swap)
        sums[iteration, chip] = mine[iteration, kept, :] + pair[iteration]
        copies = [
            start_copy(
                sums.at[iteration, chip],
                sums.at[iteration, chip],
                sum_send.at[iteration, i],
                sum_recv.at[iteration, i],
                peer,
            )
            for i, peer in enumerate(chip_peers)
        ]
        for copy in copies:
            copy.wait_recv()
        pending += copies
        total = sums[iteration, 0]
        for at in range(1, chips):
            total = total + sums[iteration, at]

        def lanes_of(array, at):
            return pltpu.roll(array, LANES - at * dirs, 1) if at else array

        gains = near_gain[kept, :]
        current = [
            tuple(lanes_of(gains, part * 4 + entry) for part in range(2)) for entry in range(4)
        ]
        gathered = [
            tuple(lanes_of(total[:, 0:LANES], part * 4 + entry) for part in range(2))
            for entry in range(4)
        ]
        upper_diag, lower_diag, cross_real, cross_imag = (
            lanes_of(total[:, LANES : 2 * LANES], at) for at in range(4)
        )
        nothing = jnp.zeros_like(upper_diag)
        hermitian = [
            (upper_diag, nothing),
            (cross_real, cross_imag),
            (cross_real, -cross_imag),
            (lower_diag, nothing),
        ]
        numerator = [
            cadd(a, b) for a, b in zip(gathered, mat_mul(current, hermitian))
        ]
        upper_diag = upper_diag + ridge_term
        lower_diag = lower_diag + ridge_term
        determinant = (
            upper_diag * lower_diag - cross_real * cross_real - cross_imag * cross_imag
        )
        inverse = [
            (lower_diag / determinant, nothing),
            (-cross_real / determinant, -cross_imag / determinant),
            (-cross_real / determinant, cross_imag / determinant),
            (upper_diag / determinant, nothing),
        ]
        estimate = mat_mul(numerator, inverse)
        updated = jnp.zeros((half, LANES), jnp.float32)
        for entry in range(4):
            for part in range(2):
                at = part * 4 + entry
                value = 0.5 * (current[entry][part] + estimate[entry][part])
                moved = pltpu.roll(value, at * dirs, 1) if at else value
                inside = near_lane[0:half] // dirs == at
                updated = jnp.where(inside, moved, updated)
        fresh[iteration] = updated

        last = iteration == ITERS - 1
        here = spread.at[iteration, group, core]
        spread[iteration, group, core] = updated
        swap = start_copy(
            fresh.at[iteration], here, turn_send.at[iteration], turn_recv.at[iteration], sibling
        )
        copies = [swap]
        if not last:
            for way, peers in enumerate((stn_peers, cross_peers)):
                copies += [
                    start_copy(
                        fresh.at[iteration],
                        here,
                        fresh_send.at[iteration, way, i],
                        fresh_recv.at[iteration, way, i],
                        peer,
                    )
                    for i, peer in enumerate(peers)
                ]
        for copy in copies:
            copy.wait_recv()
        pending += copies
        near_gain[...] = spread[iteration, group].reshape(members, LANES)
        if not last:
            turned = jnp.transpose(spread[iteration].reshape(stations, LANES))
            gain_far[...] = turned

    residual[...] = misfit[...]
    square[0:members, :] = near_gain[...]
    final[...] = jnp.transpose(square[...])[:, 0:members]
    for copy in pending:
        copy.wait_send()


def on_device(
    positions, catalogue, cluster_ids, counts, flag_mask, thermal_noise, true_gains, start_gains
):
    groups = lax.axis_size("stn")
    chans = lax.axis_size("chan")
    dirs, slots = cluster_ids.shape
    members = positions.shape[1]
    stations = groups * members
    entries = chans * catalogue.shape[1]
    chips = chans // 2
    half = members // 2
    sizes = (groups, chans, dirs, slots, members, float(chans))
    f32 = jnp.float32
    vmem = pl.BlockSpec(memory_space=pltpu.VMEM)
    smem = pl.BlockSpec(memory_space=pltpu.SMEM)
    dma = pltpu.SemaphoreType.DMA

    final, residual = pl.pallas_call(
        lambda *refs: kernel(sizes, *refs),
        name="calibrate",
        out_shape=(
            jax.ShapeDtypeStruct((8 * dirs, members), f32),
            jax.ShapeDtypeStruct((8, members, stations), f32),
        ),
        in_specs=[vmem, vmem, vmem, smem, vmem, vmem, vmem, vmem],
        out_specs=(vmem, vmem),
        scratch_shapes=[
            pltpu.VMEM((LANES, LANES), f32),
            pltpu.VMEM((dirs, slots, entries), jnp.bfloat16),
            pltpu.VMEM((catalogue.shape[1], LANES), f32),
            pltpu.VMEM((chans, catalogue.shape[1], LANES), f32),
            pltpu.VMEM((entries, LANES), jnp.bfloat16),
            pltpu.VMEM((8, LANES), f32),
            pltpu.VMEM((groups, 8, LANES), f32),
            pltpu.VMEM((8, stations), f32),
            pltpu.VMEM((members, 2 * LANES), f32),
            pltpu.VMEM((groups, members, 2 * LANES), f32),
            pltpu.VMEM((8 * dirs, stations), f32),
            pltpu.VMEM((8 * dirs, stations), f32),
            pltpu.VMEM((members, LANES), f32),
            pltpu.VMEM((members, LANES), f32),
            pltpu.VMEM((dirs, 8, members, stations), f32),
            pltpu.VMEM((dirs, 8, members, stations), f32),
            pltpu.VMEM((8, members, stations), f32),
            pltpu.VMEM((8, members, stations), f32),
            pltpu.VMEM((members, stations), f32),
            pltpu.VMEM((8, members, stations), f32),
            pltpu.VMEM((members, LANES), f32),
            pltpu.VMEM((members, LANES), f32),
            pltpu.VMEM((ITERS, half, 2 * LANES), f32),
            pltpu.VMEM((ITERS, members, 2 * LANES), f32),
            pltpu.VMEM((ITERS, chips, half, 2 * LANES), f32),
            pltpu.VMEM((ITERS, half, LANES), f32),
            pltpu.VMEM((ITERS, groups, 2, half, LANES), f32),
            dma((chans - 1,)),
            dma((chans - 1,)),
            dma((groups - 1,)),
            dma((groups - 1,)),
            dma((groups - 1,)),
            dma((groups - 1,)),
            dma((ITERS,)),
            dma((ITERS,)),
            dma((ITERS, chips - 1)),
            dma((ITERS, chips - 1)),
            dma((ITERS, 2, groups - 1)),
            dma((ITERS, 2, groups - 1)),
            dma((ITERS,)),
            dma((ITERS,)),
        ],
        compiler_params=pltpu.CompilerParams(
            collective_id=1, has_side_effects=True, vmem_limit_bytes=40 << 20
        ),
    )(
        positions,
        catalogue,
        cluster_ids,
        counts,
        flag_mask.reshape(members, stations),
        thermal_noise.reshape(8, members, stations),
        true_gains.reshape(8 * dirs, members),
        start_gains.reshape(8 * dirs, members),
    )
    return (final.reshape(true_gains.shape), residual.reshape(thermal_noise.shape))


def solution(mesh):
    return jax.shard_map(
        on_device,
        mesh=mesh,
        in_specs=(
            P(None, "stn"),
            P(None, "chan"),
            P(),
            P(),
            P("chan", "stn", None),
            P(None, None, "chan", "stn", None),
            P(None, None, None, "stn"),
            P(None, None, None, "stn"),
        ),
        out_specs=(P(None, None, None, "stn"), P(None, None, "chan", "stn", None)),
        check_vma=False,
    )
```

time: 625 us -> 107 us (0.17)
  the two profiles are of different devices: /device:TPU:64 before, /device:TPU:1 now
where the time goes in v1:
time: 107 us
  Pallas kernels  100 us (93%)
  local copies, waits for them, and re-layouts  5.96 us (6%)
    pallas_call x1, Pallas kernels, on_device(): pl.pallas_call(lambda *refs: kernel(sizes, *refs), name='calibrate', out_...  100 us
    unnamed x18, local copies, waits for them, and re-layouts  5.96 us

profile of v1, /device:TPU:1, one launch (start us, length us, event | category | flops | bytes accessed | tf_op | source)
XLA Modules:
  0.0 107.0 jit_solution(13422209681647071680)
XLA Ops:
  0.6 0.0 copy-start.5
  0.6 0.0 copy-start.6
  0.7 0.0 copy-start.7
  0.7 0.7 copy-done.5
  1.3 0.0 copy-done.6
  1.3 0.0 copy-done.7
  1.3 0.0 copy-start
  1.3 0.9 copy-done
  2.2 0.0 copy-start.1
  2.2 0.8 copy-done.1
  3.1 0.0 copy-start.2
  3.1 0.8 copy-done.2
  3.9 0.0 copy-start.3
  3.9 0.7 copy-done.3
  4.6 0.0 copy-start.4
  4.6 0.7 copy-done.4
  5.3 100.3 %calibrate.1 = (f32[128,16]{1,0:T(8,128)S(1)}, f32[8,16,256]{2,1,0:T(8,128)S(1)}) custom-call(f32[3,16]{1,0:T(4,128)S(1)} %copy-done.6, f32[7,32]{1,0:T(8,128)S(1)} %copy-done.5, s32[16,64]{1,0:T(8,128)S(1)} %copy-done.4, s32[16]{0:T(128)S(1)} %copy-done.7, s32[16,256]{1,0:T(8,128)S(1)} %bitcast.13, f32[8,16,256]{2,1,0:T(8,128)S(1)} %bitcast.8, ...), custom_call_target="tpu_custom_call" | custom-call | tf_op jit(solution)/shard_map/calibrate/pallas_call | solution.py:562
  105.7 0.6 copy.13
  106.3 0.7 copy.14
Async XLA Ops:
  0.6 0.7 copy-start.5
  0.6 0.7 copy-start.6
  0.7 0.7 copy-start.7
  1.3 0.9 copy-start
  2.2 0.8 copy-start.1
  3.1 0.8 copy-start.2
  3.9 0.7 copy-start.3
  4.6 0.7 copy-start.4

commit v2 on v1

--- a/solution.py
+++ b/solution.py
@@ -88,23 +88,44 @@
     return copy
 
 
+def far_first(count, stride):
+    ring = count // 2
+    moves = [(row, step) for row in range(2) for step in range(ring) if row or step]
+    return sorted(moves, key=lambda move: -(move[0] * stride + min(move[1], ring - move[1])))
+
+
+def moved_to(index, move, count):
+    ring = count // 2
+    row = lax.rem(index // ring + move[0], 2)
+    return row * ring + lax.rem(lax.rem(index, ring) + move[1], ring)
+
+
 def kernel(
     sizes,
+    positions_in,
+    catalogue_in,
+    ids_in,
+    counts_in,
+    flags_in,
+    noise_in,
+    true_in,
+    start_in,
+    final,
+    residual,
     positions,
     catalogue,
     ids,
     counts,
     flags,
-    noise,
     true_gains,
     start_gains,
-    final,
-    residual,
+    load_sem,
     square,
-    onehot,
     own_cat,
+    sibling_cat,
     every_cat,
     parts_cat,
+    cat_pair_sem,
     own_place,
     every_place,
     place_rows,
@@ -149,54 +170,79 @@
     chip = channel // 2
     core = lax.rem(channel, 2)
     stations = groups * members
-    entries = chans * catalogue.shape[1]
     half = members // 2
 
-    chan_peers = [{"chan": lax.rem(channel + step, chans)} for step in range(1, chans)]
-    stn_peers = [{"stn": lax.rem(group + step, groups)} for step in range(1, groups)]
+    loads = [
+        pltpu.make_async_copy(source, target, load_sem.at[i])
+        for i, (source, target) in enumerate(
+            (
+                (catalogue_in, catalogue),
+                (positions_in, positions),
+                (true_in, true_gains),
+                (start_in, start_gains),
+                (ids_in, ids),
+                (counts_in, counts),
+                (flags_in, flags),
+                (noise_in, observed),
+            )
+        )
+    ]
+    for load in loads:
+        load.start()
+
     sibling = {"chan": chip * 2 + 1 - core}
-    chip_peers = [{"chan": lax.rem(chip + step, chips) * 2 + core} for step in range(1, chips)]
-    cross_peers = [
-        {"stn": lax.rem(group + step, groups), "chan": chip * 2 + 1 - core}
-        for step in range(1, groups)
-    ]
+    chip_moves = [moved_to(chip, move, chips) for move in far_first(chips, 2)]
+    chip_peers = [{"chan": peer * 2 + core} for peer in chip_moves]
+    group_moves = [moved_to(group, move, groups) for move in far_first(groups, 1)]
+    stn_peers = [{"stn": peer} for peer in group_moves]
+    cross_peers = [{"stn": peer, "chan": chip * 2 + 1 - core} for peer in group_moves]
 
     barrier = pltpu.get_barrier_semaphore()
-    greeted = chan_peers + stn_peers + cross_peers
+    greeted = chip_peers + stn_peers + cross_peers + [sibling]
     for peer in greeted:
         pl.semaphore_signal(barrier, inc=1, device_id=peer, device_id_type=MESH)
 
-    square[...] = jnp.zeros_like(square)
-    for copy_at in range(3):
-        square[32 * copy_at : 32 * copy_at + 7, 0 : catalogue.shape[1]] = catalogue[...]
-    own_cat[...] = jnp.transpose(square[...])[0 : catalogue.shape[1], :]
+    cat_width = catalogue.shape[1]
+    for load in loads[0:2]:
+        load.wait()
+    own_cat[...] = jnp.zeros_like(own_cat)
+    own_cat[0:7, 0:cat_width] = catalogue[...]
+    own_cat[...] = jnp.where(core == 0, own_cat[...], pltpu.roll(own_cat[...], cat_width, 1))
+    own_place[...] = jnp.zeros_like(own_place)
+    own_place[0:3, 0:members] = positions[...]
+    for load in loads[2:4]:
+        load.wait()
     square[...] = jnp.zeros_like(square)
     square[:, 0:members] = true_gains[...]
     own_gains[:, 0:LANES] = jnp.transpose(square[...])[0:members, :]
     square[:, 0:members] = start_gains[...]
     own_gains[:, LANES : 2 * LANES] = jnp.transpose(square[...])[0:members, :]
-    own_place[...] = jnp.zeros_like(own_place)
-    own_place[0:3, 0:members] = positions[...]
 
     pl.semaphore_wait(barrier, len(greeted))
 
-    cat_copies = [
-        start_copy(own_cat, every_cat.at[channel], cat_send.at[i], cat_recv.at[i], peer)
-        for i, peer in enumerate(chan_peers)
-    ]
+    cat_swap = start_copy(own_cat, sibling_cat, cat_pair_sem.at[0], cat_pair_sem.at[1], sibling)
     place_copies = [
         start_copy(own_place, every_place.at[group], place_send.at[i], place_recv.at[i], peer)
         for i, peer in enumerate(stn_peers)
+    ]
+    cat_swap.wait_recv()
+    every_cat[chip] = own_cat[...] + sibling_cat[...]
+    cat_copies = [
+        start_copy(
+            every_cat.at[chip], every_cat.at[chip], cat_send.at[i], cat_recv.at[i], peer
+        )
+        for i, peer in enumerate(chip_peers)
     ]
     gain_copies = [
         start_copy(own_gains, every_gains.at[group], gain_send.at[i], gain_recv.at[i], peer)
         for i, peer in enumerate(stn_peers)
     ]
-    every_cat[channel] = own_cat[...]
     every_place[group] = own_place[...]
     every_gains[group] = own_gains[...]
     near_true[...] = own_gains[:, 0:LANES]
     near_gain[...] = own_gains[:, LANES : 2 * LANES]
+    for load in loads[4:]:
+        load.wait()
 
     near_index = group * members + lax.broadcasted_iota(jnp.int32, (members, stations), 0)
     far_index = lax.broadcasted_iota(jnp.int32, (members, stations), 1)
@@ -204,19 +250,9 @@
 
     square[...] = jnp.zeros_like(square)
     square[0:dirs, 0:slots] = ids[...].astype(jnp.float32)
-    ids_turned = jnp.transpose(square[...])[0:slots, :]
-    square[0:slots, :] = ids_turned
+    square[...] = jnp.transpose(square[...])
     lane_column = lax.broadcasted_iota(jnp.int32, (slots, LANES), 1)
-    entry_at = lax.broadcasted_iota(jnp.int32, (slots, entries), 1).astype(jnp.float32)
-
-    def mark(direction, carry):
-        named = jnp.sum(
-            jnp.where(lane_column == direction, square[0:slots, :], 0.0), axis=1, keepdims=True
-        )
-        onehot[direction] = jnp.where(named == entry_at, 1.0, 0.0).astype(jnp.bfloat16)
-        return carry
-
-    lax.fori_loop(0, dirs, mark, 0)
+    lane_value = lane_column.astype(jnp.float32)
 
     frequency = 1.0 + band_spread * channel.astype(jnp.float32) / chan_total
     log_frequency = jnp.log(jnp.full((1, LANES), frequency, jnp.float32))
@@ -226,14 +262,20 @@
 
     for copy in cat_copies:
         copy.wait_recv()
-    whole = every_cat[...].reshape(entries, LANES)
+    stacked = jnp.concatenate(
+        [
+            every_cat[2 * at] + pltpu.roll(every_cat[2 * at + 1], 2 * cat_width, 1)
+            for at in range(chips // 2)
+        ]
+        + [jnp.zeros((LANES - 4 * chips, LANES), jnp.float32)],
+        axis=0,
+    )
+    whole = jnp.transpose(stacked)
     first = whole.astype(jnp.bfloat16).astype(jnp.float32)
     second = (whole - first).astype(jnp.bfloat16).astype(jnp.float32)
     third = whole - first - second
-    wide_lane = lax.broadcasted_iota(jnp.int32, (entries, LANES), 1)
-    parts_cat[...] = jnp.where(
-        wide_lane < 32, first, jnp.where(wide_lane < 64, second, third)
-    ).astype(jnp.bfloat16)
+    parts_cat[:, 0:LANES] = (first + pltpu.roll(second, 64, 1)).astype(jnp.bfloat16)
+    parts_cat[:, LANES : 2 * LANES] = third.astype(jnp.bfloat16)
 
     for copy in place_copies:
         copy.wait_recv()
@@ -249,16 +291,32 @@
         tiled = tiled + pltpu.roll(tiled, shift, 1)
 
     def model(direction, carry):
-        picked = lax.dot_general(
-            onehot[direction],
+        named = jnp.sum(
+            jnp.where(lane_column == direction, square[0:slots, :], 0.0), axis=1, keepdims=True
+        )
+        block_of = jnp.floor(named * (1.0 / LANES))
+        within = named - block_of * LANES
+        picked = jnp.dot(
+            jnp.where(within == lane_value, 1.0, 0.0).astype(jnp.bfloat16),
             parts_cat[...],
-            (((1,), (0,)), ((), ())),
             preferred_element_type=jnp.float32,
         )
-        picked = picked + pltpu.roll(picked, LANES - 32, 1) + pltpu.roll(picked, LANES - 64, 1)
+        picked = (
+            picked[:, 0:LANES]
+            + pltpu.roll(picked[:, 0:LANES], 64, 1)
+            + picked[:, LANES : 2 * LANES]
+        )
+        lane_wanted = block_of * 8.0
 
         def column(at):
-            return jnp.broadcast_to(picked[:, at : at + 1], (slots, LANES))
+            return jnp.broadcast_to(
+                jnp.sum(
+                    jnp.where(lane_value == lane_wanted + float(at), picked, 0.0),
+                    axis=1,
+                    keepdims=True,
+                ),
+                (slots, LANES),
+            )
 
         cos_l, cos_m = column(0), column(1)
         depth = jnp.sqrt(1.0 - cos_l * cos_l - cos_m * cos_m) - 1.0
@@ -308,7 +366,7 @@
         coherent[direction] = result.reshape(8, members, stations)
         return carry
 
-    lax.fori_loop(0, dirs, model, 0)
+    lax.fori_loop(0, dirs, model, 0, unroll=4)
 
     for copy in gain_copies:
         copy.wait_recv()
@@ -354,8 +412,6 @@
             for part in range(2):
                 ref[part * 4 + entry, :, lanes] += matrix[entry][part]
 
-    observed[...] = noise[...]
-
     def observe(direction, carry):
         near = near_matrix(near_true, direction)
         for lanes in halves:
@@ -365,7 +421,7 @@
             add_planes(observed, lanes, mat_mul(near, spun))
         return carry
 
-    lax.fori_loop(0, dirs, observe, 0)
+    lax.fori_loop(0, dirs, observe, 0, unroll=2)
 
     def predict(direction, carry):
         near = near_matrix(near_gain, direction)
@@ -420,7 +476,7 @@
         cross_sum[...] = collected
         return carry
 
-    pending = cat_copies + place_copies + gain_copies
+    pending = [cat_swap] + cat_copies + place_copies + gain_copies
     kept = pl.ds(pl.multiple_of(core * half, half), half)
     away = pl.ds(pl.multiple_of((1 - core) * half, half), half)
     cross_sum[...] = jnp.zeros_like(cross_sum)
@@ -428,10 +484,10 @@
 
     for iteration in range(ITERS):
         predicted[...] = jnp.zeros_like(predicted)
-        lax.fori_loop(0, dirs, predict, 0)
+        lax.fori_loop(0, dirs, predict, 0, unroll=2)
         for plane in range(8):
             misfit[plane] = weight[...] * (observed[plane] - predicted[plane])
-        lax.fori_loop(0, dirs, correlate, 0)
+        lax.fori_loop(0, dirs, correlate, 0, unroll=2)
         mine[iteration, :, 0:LANES] = cross_sum[...]
         mine[iteration, :, LANES : 2 * LANES] = normal[...]
 
@@ -516,17 +572,17 @@
         )
         copies = [swap]
         if not last:
-            for way, peers in enumerate((stn_peers, cross_peers)):
-                copies += [
-                    start_copy(
-                        fresh.at[iteration],
-                        here,
-                        fresh_send.at[iteration, way, i],
-                        fresh_recv.at[iteration, way, i],
-                        peer,
-                    )
-                    for i, peer in enumerate(peers)
-                ]
+            copies += [
+                start_copy(
+                    fresh.at[iteration],
+                    here,
+                    fresh_send.at[iteration, way, i],
+                    fresh_recv.at[iteration, way, i],
+                    peer,
+                )
+                for i, both in enumerate(zip(stn_peers, cross_peers))
+                for way, peer in enumerate(both)
+            ]
         for copy in copies:
             copy.wait_recv()
         pending += copies
@@ -550,13 +606,12 @@
     dirs, slots = cluster_ids.shape
     members = positions.shape[1]
     stations = groups * members
-    entries = chans * catalogue.shape[1]
     chips = chans // 2
     half = members // 2
     sizes = (groups, chans, dirs, slots, members, float(chans))
     f32 = jnp.float32
     vmem = pl.BlockSpec(memory_space=pltpu.VMEM)
-    smem = pl.BlockSpec(memory_space=pltpu.SMEM)
+    hbm = pl.BlockSpec(memory_space=pltpu.HBM)
     dma = pltpu.SemaphoreType.DMA
 
     final, residual = pl.pallas_call(
@@ -566,14 +621,23 @@
             jax.ShapeDtypeStruct((8 * dirs, members), f32),
             jax.ShapeDtypeStruct((8, members, stations), f32),
         ),
-        in_specs=[vmem, vmem, vmem, smem, vmem, vmem, vmem, vmem],
+        in_specs=[hbm] * 8,
         out_specs=(vmem, vmem),
         scratch_shapes=[
+            pltpu.VMEM(positions.shape, f32),
+            pltpu.VMEM(catalogue.shape, f32),
+            pltpu.VMEM(cluster_ids.shape, jnp.int32),
+            pltpu.SMEM(counts.shape, jnp.int32),
+            pltpu.VMEM((members, stations), jnp.int32),
+            pltpu.VMEM((8 * dirs, members), f32),
+            pltpu.VMEM((8 * dirs, members), f32),
+            dma((8,)),
             pltpu.VMEM((LANES, LANES), f32),
-            pltpu.VMEM((dirs, slots, entries), jnp.bfloat16),
-            pltpu.VMEM((catalogue.shape[1], LANES), f32),
-            pltpu.VMEM((chans, catalogue.shape[1], LANES), f32),
-            pltpu.VMEM((entries, LANES), jnp.bfloat16),
+            pltpu.VMEM((8, LANES), f32),
+            pltpu.VMEM((8, LANES), f32),
+            pltpu.VMEM((chips, 8, LANES), f32),
+            pltpu.VMEM((LANES, 2 * LANES), jnp.bfloat16),
+            dma((2,)),
             pltpu.VMEM((8, LANES), f32),
             pltpu.VMEM((groups, 8, LANES), f32),
             pltpu.VMEM((8, stations), f32),
@@ -596,8 +660,8 @@
             pltpu.VMEM((ITERS, chips, half, 2 * LANES), f32),
             pltpu.VMEM((ITERS, half, LANES), f32),
             pltpu.VMEM((ITERS, groups, 2, half, LANES), f32),
-            dma((chans - 1,)),
-            dma((chans - 1,)),
+            dma((chips - 1,)),
+            dma((chips - 1,)),
             dma((groups - 1,)),
             dma((groups - 1,)),
             dma((groups - 1,)),
@@ -612,7 +676,7 @@
             dma((ITERS,)),
         ],
         compiler_params=pltpu.CompilerParams(
-            collective_id=1, has_side_effects=True, vmem_limit_bytes=40 << 20
+            collective_id=1, has_side_effects=True, vmem_limit_bytes=60 << 20
         ),
     )(
         positions,

time: 107 us -> 82.8 us (0.77)
  Pallas kernels: 100 us -> 79.8 us
  local copies, waits for them, and re-layouts: 5.96 us -> 2.17 us
    pallas_call x1, Pallas kernels: 100 us -> 79.8 us  [on_device(): pl.pallas_call(lambda *refs: kernel(sizes, *refs), name='calibrate', out_...]
    unnamed x18 -> x4, local copies, waits for them, and re-layouts: 5.96 us -> 2.17 us
where the time goes in v2:
time: 82.8 us; the launch traced here: 82.6 us
  Pallas kernels  79.8 us (96%)
  local copies, waits for them, and re-layouts  2.17 us (3%)
    pallas_call x1, Pallas kernels, on_device(): pl.pallas_call(lambda *refs: kernel(sizes, *refs), name='calibrate', out_...  79.8 us
    unnamed x4, local copies, waits for them, and re-layouts  2.17 us

profile of v2, /device:TPU:1, one launch (start us, length us, event | category | flops | bytes accessed | tf_op | source)
XLA Modules:
  0.0 82.6 jit_solution(17059978837917215594)
XLA Ops:
  0.6 79.8 %calibrate.1 = (f32[128,16]{1,0:T(8,128)}, f32[8,16,256]{2,1,0:T(8,128)}) custom-call(f32[3,16]{1,0:T(4,128)} %refs_0_.1, f32[7,32]{1,0:T(8,128)} %refs_1_.1, s32[16,64]{1,0:T(8,128)} %refs_2_.1, s32[16]{0:T(128)} %refs_3_.1, s32[16,256]{1,0:T(8,128)} %bitcast.13, f32[8,16,256]{2,1,0:T(8,128)} %bitcast.8, f32[128,16]{1,0:T(8,128)} %bitcast.11, ...), custom_call_target="tpu_custom_call" | custom-call | tf_op jit(solution)/shard_map/calibrate/pallas_call | solution.py:617
  80.4 0.0 copy-start
  80.4 1.5 %copy.13 = f32[2,4,16,16]{3,2,1,0:T(8,128)} copy(f32[2,4,16,16]{3,2,1,0:T(8,128)} %bitcast.10) | data formatting | bytes 16384
  81.9 0.0 copy-done
  81.9 0.7 copy.14
Async XLA Ops:
  80.4 1.5 %copy-start = (f32[8,16,256]{2,1,0:T(8,128)S(1)}, f32[8,16,256]{2,1,0:T(8,128)}, u32[]{:S(2)}) copy-start(f32[8,16,256]{2,1,0:T(8,128)} %get-tuple-element.5) | copy-start | bytes 393220

commit v3 on v2

--- a/solution.py
+++ b/solution.py
@@ -1,4 +1,4 @@
-import math
+import functools
 
 import jax
 import jax.numpy as jnp
@@ -120,6 +120,7 @@
     true_gains,
     start_gains,
     load_sem,
+    store_sem,
     square,
     own_cat,
     sibling_cat,
@@ -141,7 +142,6 @@
     predicted,
     weight,
     misfit,
-    cross_sum,
     normal,
     pair,
     mine,
@@ -195,10 +195,9 @@
     chip_peers = [{"chan": peer * 2 + core} for peer in chip_moves]
     group_moves = [moved_to(group, move, groups) for move in far_first(groups, 1)]
     stn_peers = [{"stn": peer} for peer in group_moves]
-    cross_peers = [{"stn": peer, "chan": chip * 2 + 1 - core} for peer in group_moves]
 
     barrier = pltpu.get_barrier_semaphore()
-    greeted = chip_peers + stn_peers + cross_peers + [sibling]
+    greeted = chip_peers + stn_peers + [sibling]
     for peer in greeted:
         pl.semaphore_signal(barrier, inc=1, device_id=peer, device_id_type=MESH)
 
@@ -260,7 +259,7 @@
     imag_lane = lane_row >= 4 * members
     entry_lane = lax.rem(lane_row // members, 4)
 
-    for copy in cat_copies:
+    for copy in reversed(cat_copies):
         copy.wait_recv()
     stacked = jnp.concatenate(
         [
@@ -277,7 +276,7 @@
     parts_cat[:, 0:LANES] = (first + pltpu.roll(second, 64, 1)).astype(jnp.bfloat16)
     parts_cat[:, LANES : 2 * LANES] = third.astype(jnp.bfloat16)
 
-    for copy in place_copies:
+    for copy in reversed(place_copies):
         copy.wait_recv()
     per_row = LANES // members
     scale = turn_scale * frequency
@@ -368,7 +367,7 @@
 
     lax.fori_loop(0, dirs, model, 0, unroll=4)
 
-    for copy in gain_copies:
+    for copy in reversed(gain_copies):
         copy.wait_recv()
     turned = jnp.transpose(every_gains[:, :, 0:LANES].reshape(stations, LANES))
     true_far[...] = turned
@@ -412,95 +411,122 @@
             for part in range(2):
                 ref[part * 4 + entry, :, lanes] += matrix[entry][part]
 
-    def observe(direction, carry):
-        near = near_matrix(near_true, direction)
+    def predict(step, carry, with_truth):
+        directions = [step * 2, step * 2 + 1]
+        near = [near_matrix(near_gain, direction) for direction in directions]
+        if with_truth:
+            near_sky = [near_matrix(near_true, direction) for direction in directions]
+        totals = [[0.0] * 4 for direction in directions]
         for lanes in halves:
-            spun = mat_mul_adj(
-                planes(coherent, lanes, direction), far_matrix(true_far, direction, lanes)
-            )
-            add_planes(observed, lanes, mat_mul(near, spun))
+            modelled, truth = [], []
+            for at, direction in enumerate(directions):
+                seen = planes(coherent, lanes, direction)
+                if with_truth:
+                    spun = mat_mul_adj(seen, far_matrix(true_far, direction, lanes))
+                    truth.append(mat_mul(near_sky[at], spun))
+                spun = mat_mul_adj(seen, far_matrix(gain_far, direction, lanes))
+                modelled.append(mat_mul(near[at], spun))
+                for entry in range(4):
+                    for part in range(2):
+                        product[direction, part * 4 + entry, :, lanes] = spun[entry][part]
+                weighted = [
+                    tuple(weight[:, lanes] * value for value in spun[entry]) for entry in range(2)
+                ]
+                first_power = sum(
+                    weighted[entry][part] * spun[entry][part]
+                    for entry in range(2)
+                    for part in range(2)
+                )
+                second_power = weight[:, lanes] * sum(
+                    spun[entry][part] * spun[entry][part] for entry in (2, 3) for part in range(2)
+                )
+                cross = cadd(cmul_conj(weighted[0], spun[2]), cmul_conj(weighted[1], spun[3]))
+                for kind, value in enumerate((first_power, second_power, *cross)):
+                    totals[at][kind] = totals[at][kind] + value
+            add_planes(predicted, lanes, [cadd(a, b) for a, b in zip(*modelled)])
+            if with_truth:
+                add_planes(observed, lanes, [cadd(a, b) for a, b in zip(*truth)])
+        collected = normal[...]
+        for at, direction in enumerate(directions):
+            for kind in range(4):
+                collected = jnp.where(
+                    near_lane == kind * dirs + direction,
+                    jnp.sum(totals[at][kind], axis=1, keepdims=True),
+                    collected,
+                )
+        normal[...] = collected
         return carry
 
-    lax.fori_loop(0, dirs, observe, 0, unroll=2)
-
-    def predict(direction, carry):
-        near = near_matrix(near_gain, direction)
-        totals = [0.0] * 4
-        for lanes in halves:
-            spun = mat_mul_adj(
-                planes(coherent, lanes, direction), far_matrix(gain_far, direction, lanes)
-            )
-            add_planes(predicted, lanes, mat_mul(near, spun))
+    half_lane = near_lane[0:half]
+
+    def correlate(rows, at, iteration):
+        def body(direction, carry):
+            missed = [
+                tuple(misfit[part * 4 + entry, rows, :] for part in range(2))
+                for entry in range(4)
+            ]
+            turned_back = [
+                tuple(product[direction, part * 4 + entry, rows, :] for part in range(2))
+                for entry in range(4)
+            ]
+            found = mat_mul_adj(missed, turned_back)
+            collected = mine[iteration, at, :, 0:LANES]
             for entry in range(4):
                 for part in range(2):
-                    product[direction, part * 4 + entry, :, lanes] = spun[entry][part]
-            weighted = [
-                tuple(weight[:, lanes] * value for value in spun[entry]) for entry in range(2)
-            ]
-            first_power = sum(
-                weighted[entry][part] * spun[entry][part]
-                for entry in range(2)
-                for part in range(2)
-            )
-            second_power = weight[:, lanes] * sum(
-                spun[entry][part] * spun[entry][part] for entry in (2, 3) for part in range(2)
-            )
-            cross = cadd(cmul_conj(weighted[0], spun[2]), cmul_conj(weighted[1], spun[3]))
-            for at, value in enumerate((first_power, second_power, *cross)):
-                totals[at] = totals[at] + value
-        collected = normal[...]
-        for at in range(4):
-            collected = jnp.where(
-                near_lane == at * dirs + direction,
-                jnp.sum(totals[at], axis=1, keepdims=True),
-                collected,
-            )
-        normal[...] = collected
-        return carry
-
-    def correlate(direction, carry):
-        totals = [[0.0, 0.0] for entry in range(4)]
-        for lanes in halves:
-            found = mat_mul_adj(planes(misfit, lanes), planes(product, lanes, direction))
-            for entry in range(4):
-                for part in range(2):
-                    totals[entry][part] = totals[entry][part] + found[entry][part]
-        collected = cross_sum[...]
-        for entry in range(4):
-            for part in range(2):
-                collected = jnp.where(
-                    near_lane == (part * 4 + entry) * dirs + direction,
-                    jnp.sum(totals[entry][part], axis=1, keepdims=True),
-                    collected,
-                )
-        cross_sum[...] = collected
-        return carry
+                    value = sum(found[entry][part][:, lanes] for lanes in halves)
+                    collected = jnp.where(
+                        half_lane == (part * 4 + entry) * dirs + direction,
+                        jnp.sum(value, axis=1, keepdims=True),
+                        collected,
+                    )
+            mine[iteration, at, :, 0:LANES] = collected
+            return carry
+
+        mine[iteration, at] = jnp.zeros((half, 2 * LANES), jnp.float32)
+        lax.fori_loop(0, dirs, body, 0, unroll=4)
+        mine[iteration, at, :, LANES : 2 * LANES] = normal[rows, :]
 
     pending = [cat_swap] + cat_copies + place_copies + gain_copies
+
+    def settle(copies):
+        for copy in pending:
+            copy.wait_send()
+        pending.clear()
+        for copy in reversed(copies):
+            copy.wait_recv()
+        pending.extend(copies)
     kept = pl.ds(pl.multiple_of(core * half, half), half)
     away = pl.ds(pl.multiple_of((1 - core) * half, half), half)
-    cross_sum[...] = jnp.zeros_like(cross_sum)
     normal[...] = jnp.zeros_like(normal)
 
     for iteration in range(ITERS):
         predicted[...] = jnp.zeros_like(predicted)
-        lax.fori_loop(0, dirs, predict, 0, unroll=2)
+        lax.fori_loop(
+            0,
+            dirs // 2,
+            functools.partial(predict, with_truth=iteration == 0),
+            0,
+            unroll=1,
+        )
         for plane in range(8):
             misfit[plane] = weight[...] * (observed[plane] - predicted[plane])
-        lax.fori_loop(0, dirs, correlate, 0, unroll=2)
-        mine[iteration, :, 0:LANES] = cross_sum[...]
-        mine[iteration, :, LANES : 2 * LANES] = normal[...]
-
+        last = iteration == ITERS - 1
+        if last:
+            store = pltpu.make_async_copy(misfit, residual, store_sem)
+            store.start()
+
+        correlate(away, 0, iteration)
         swap = start_copy(
-            mine.at[iteration, away],
+            mine.at[iteration, 0],
             pair.at[iteration],
             pair_send.at[iteration],
             pair_recv.at[iteration],
             sibling,
         )
+        correlate(kept, 1, iteration)
         swap.wait_recv()
         pending.append(swap)
-        sums[iteration, chip] = mine[iteration, kept, :] + pair[iteration]
+        sums[iteration, chip] = mine[iteration, 1] + pair[iteration]
         copies = [
             start_copy(
                 sums.at[iteration, chip],
@@ -511,9 +537,7 @@
             )
             for i, peer in enumerate(chip_peers)
         ]
-        for copy in copies:
-            copy.wait_recv()
-        pending += copies
+        settle(copies)
         total = sums[iteration, 0]
         for at in range(1, chips):
             total = total + sums[iteration, at]
@@ -564,36 +588,48 @@
                 updated = jnp.where(inside, moved, updated)
         fresh[iteration] = updated
 
-        last = iteration == ITERS - 1
-        here = spread.at[iteration, group, core]
-        spread[iteration, group, core] = updated
-        swap = start_copy(
-            fresh.at[iteration], here, turn_send.at[iteration], turn_recv.at[iteration], sibling
-        )
-        copies = [swap]
+        spread[iteration, core, group] = updated
         if not last:
-            copies += [
+            settle(
+                [
+                    start_copy(
+                        fresh.at[iteration],
+                        spread.at[iteration, core, group],
+                        fresh_send.at[iteration, i],
+                        fresh_recv.at[iteration, i],
+                        peer,
+                    )
+                    for i, peer in enumerate(stn_peers)
+                ]
+            )
+            handed = spread.at[iteration, core]
+        else:
+            handed = spread.at[iteration, core, group]
+        settle(
+            [
                 start_copy(
-                    fresh.at[iteration],
-                    here,
-                    fresh_send.at[iteration, way, i],
-                    fresh_recv.at[iteration, way, i],
-                    peer,
+                    handed, handed, turn_send.at[iteration], turn_recv.at[iteration], sibling
                 )
-                for i, both in enumerate(zip(stn_peers, cross_peers))
-                for way, peer in enumerate(both)
             ]
-        for copy in copies:
-            copy.wait_recv()
-        pending += copies
-        near_gain[...] = spread[iteration, group].reshape(members, LANES)
+        )
+        near_gain[...] = jnp.concatenate(
+            [spread[iteration, at, group] for at in range(2)], axis=0
+        )
         if not last:
-            turned = jnp.transpose(spread[iteration].reshape(stations, LANES))
-            gain_far[...] = turned
-
-    residual[...] = misfit[...]
+            gain_far[...] = jnp.transpose(
+                jnp.concatenate(
+                    [
+                        spread[iteration, at, other]
+                        for other in range(groups)
+                        for at in range(2)
+                    ],
+                    axis=0,
+                )
+            )
+
     square[0:members, :] = near_gain[...]
     final[...] = jnp.transpose(square[...])[:, 0:members]
+    store.wait()
     for copy in pending:
         copy.wait_send()
 
@@ -622,7 +658,7 @@
             jax.ShapeDtypeStruct((8, members, stations), f32),
         ),
         in_specs=[hbm] * 8,
-        out_specs=(vmem, vmem),
+        out_specs=(vmem, hbm),
         scratch_shapes=[
             pltpu.VMEM(positions.shape, f32),
             pltpu.VMEM(catalogue.shape, f32),
@@ -632,6 +668,7 @@
             pltpu.VMEM((8 * dirs, members), f32),
             pltpu.VMEM((8 * dirs, members), f32),
             dma((8,)),
+            dma,
             pltpu.VMEM((LANES, LANES), f32),
             pltpu.VMEM((8, LANES), f32),
             pltpu.VMEM((8, LANES), f32),
@@ -654,12 +691,11 @@
             pltpu.VMEM((members, stations), f32),
             pltpu.VMEM((8, members, stations), f32),
             pltpu.VMEM((members, LANES), f32),
-            pltpu.VMEM((members, LANES), f32),
             pltpu.VMEM((ITERS, half, 2 * LANES), f32),
-            pltpu.VMEM((ITERS, members, 2 * LANES), f32),
+            pltpu.VMEM((ITERS, 2, half, 2 * LANES), f32),
             pltpu.VMEM((ITERS, chips, half, 2 * LANES), f32),
             pltpu.VMEM((ITERS, half, LANES), f32),
-            pltpu.VMEM((ITERS, groups, 2, half, LANES), f32),
+            pltpu.VMEM((ITERS, 2, groups, half, LANES), f32),
             dma((chips - 1,)),
             dma((chips - 1,)),
             dma((groups - 1,)),
@@ -670,8 +706,8 @@
             dma((ITERS,)),
             dma((ITERS, chips - 1)),
             dma((ITERS, chips - 1)),
-            dma((ITERS, 2, groups - 1)),
-            dma((ITERS, 2, groups - 1)),
+            dma((ITERS, groups - 1)),
+            dma((ITERS, groups - 1)),
             dma((ITERS,)),
             dma((ITERS,)),
         ],

time: 82.8 us -> 80.4 us (0.971)
  Pallas kernels: 79.8 us -> 77.4 us
    pallas_call x1, Pallas kernels: 79.8 us -> 77.4 us  [on_device(): pl.pallas_call(lambda *refs: kernel(sizes, *refs), name='calibrate', out_...]
where the time goes in v3:
time: 80.4 us; the launch traced here: 80.3 us
  Pallas kernels  77.4 us (96%)
  local copies, waits for them, and re-layouts  2.17 us (3%)
    pallas_call x1, Pallas kernels, on_device(): pl.pallas_call(lambda *refs: kernel(sizes, *refs), name='calibrate', out_...  77.4 us
    unnamed x4, local copies, waits for them, and re-layouts  2.17 us

profile of v3, /device:TPU:1, one launch (start us, length us, event | category | flops | bytes accessed | tf_op | source)
XLA Modules:
  0.0 80.3 jit_solution(14566592840792695876)
XLA Ops:
  0.6 77.4 %calibrate.1 = (f32[128,16]{1,0:T(8,128)}, f32[8,16,256]{2,1,0:T(8,128)}) custom-call(f32[3,16]{1,0:T(4,128)} %refs_0_.1, f32[7,32]{1,0:T(8,128)} %refs_1_.1, s32[16,64]{1,0:T(8,128)} %refs_2_.1, s32[16]{0:T(128)} %refs_3_.1, s32[16,256]{1,0:T(8,128)} %bitcast.13, f32[8,16,256]{2,1,0:T(8,128)} %bitcast.8, f32[128,16]{1,0:T(8,128)} %bitcast.11, ...), custom_call_target="tpu_custom_call" | custom-call | tf_op jit(solution)/shard_map/calibrate/pallas_call | solution.py:653
  78.1 0.0 copy-start
  78.1 1.5 %copy.13 = f32[2,4,16,16]{3,2,1,0:T(8,128)} copy(f32[2,4,16,16]{3,2,1,0:T(8,128)} %bitcast.10) | data formatting | bytes 16384
  79.6 0.0 copy-done
  79.6 0.7 copy.14
Async XLA Ops:
  78.1 1.5 %copy-start = (f32[8,16,256]{2,1,0:T(8,128)S(1)}, f32[8,16,256]{2,1,0:T(8,128)}, u32[]{:S(2)}) copy-start(f32[8,16,256]{2,1,0:T(8,128)} %get-tuple-element.5) | copy-start | bytes 393220

commit v4 on v3

--- a/solution.py
+++ b/solution.py
@@ -120,12 +120,13 @@
     true_gains,
     start_gains,
     load_sem,
-    store_sem,
     square,
     own_cat,
     sibling_cat,
     every_cat,
     parts_cat,
+    onehot,
+    picks,
     cat_pair_sem,
     own_place,
     every_place,
@@ -209,14 +210,6 @@
     own_cat[...] = jnp.where(core == 0, own_cat[...], pltpu.roll(own_cat[...], cat_width, 1))
     own_place[...] = jnp.zeros_like(own_place)
     own_place[0:3, 0:members] = positions[...]
-    for load in loads[2:4]:
-        load.wait()
-    square[...] = jnp.zeros_like(square)
-    square[:, 0:members] = true_gains[...]
-    own_gains[:, 0:LANES] = jnp.transpose(square[...])[0:members, :]
-    square[:, 0:members] = start_gains[...]
-    own_gains[:, LANES : 2 * LANES] = jnp.transpose(square[...])[0:members, :]
-
     pl.semaphore_wait(barrier, len(greeted))
 
     cat_swap = start_copy(own_cat, sibling_cat, cat_pair_sem.at[0], cat_pair_sem.at[1], sibling)
@@ -232,6 +225,14 @@
         )
         for i, peer in enumerate(chip_peers)
     ]
+    for load in loads[2:4]:
+        load.wait()
+    square[...] = jnp.zeros_like(square)
+    square[:, 0:members] = true_gains[...]
+    own_gains[:, 0:LANES] = jnp.transpose(square[...])[0:members, :]
+    square[:, 0:members] = start_gains[...]
+    own_gains[:, LANES : 2 * LANES] = jnp.transpose(square[...])[0:members, :]
+
     gain_copies = [
         start_copy(own_gains, every_gains.at[group], gain_send.at[i], gain_recv.at[i], peer)
         for i, peer in enumerate(stn_peers)
@@ -252,6 +253,19 @@
     square[...] = jnp.transpose(square[...])
     lane_column = lax.broadcasted_iota(jnp.int32, (slots, LANES), 1)
     lane_value = lane_column.astype(jnp.float32)
+    lane_block = (lane_column // 8).astype(jnp.float32)
+
+    def mark(direction, carry):
+        named = jnp.sum(
+            jnp.where(lane_column == direction, square[0:slots, :], 0.0), axis=1, keepdims=True
+        )
+        block_of = jnp.floor(named * (1.0 / LANES))
+        within = named - block_of * LANES
+        onehot[direction] = jnp.where(within == lane_value, 1.0, 0.0).astype(jnp.bfloat16)
+        picks[direction] = jnp.where(lane_block == block_of, 1.0, 0.0)
+        return carry
+
+    lax.fori_loop(0, dirs, mark, 0, unroll=4)
 
     frequency = 1.0 + band_spread * channel.astype(jnp.float32) / chan_total
     log_frequency = jnp.log(jnp.full((1, LANES), frequency, jnp.float32))
@@ -275,6 +289,17 @@
     third = whole - first - second
     parts_cat[:, 0:LANES] = (first + pltpu.roll(second, 64, 1)).astype(jnp.bfloat16)
     parts_cat[:, LANES : 2 * LANES] = third.astype(jnp.bfloat16)
+
+    found = jnp.dot(
+        onehot[...].reshape(dirs * slots, LANES),
+        parts_cat[...],
+        preferred_element_type=jnp.float32,
+    )
+    found = (
+        found[:, 0:LANES] + pltpu.roll(found[:, 0:LANES], 64, 1) + found[:, LANES : 2 * LANES]
+    )
+    picks[...] = picks[...] * found.reshape(dirs, slots, LANES)
+    lane_kind = lax.rem(lane_column, 8)
 
     for copy in reversed(place_copies):
         copy.wait_recv()
@@ -290,27 +315,12 @@
         tiled = tiled + pltpu.roll(tiled, shift, 1)
 
     def model(direction, carry):
-        named = jnp.sum(
-            jnp.where(lane_column == direction, square[0:slots, :], 0.0), axis=1, keepdims=True
-        )
-        block_of = jnp.floor(named * (1.0 / LANES))
-        within = named - block_of * LANES
-        picked = jnp.dot(
-            jnp.where(within == lane_value, 1.0, 0.0).astype(jnp.bfloat16),
-            parts_cat[...],
-            preferred_element_type=jnp.float32,
-        )
-        picked = (
-            picked[:, 0:LANES]
-            + pltpu.roll(picked[:, 0:LANES], 64, 1)
-            + picked[:, LANES : 2 * LANES]
-        )
-        lane_wanted = block_of * 8.0
+        picked = picks[direction]
 
         def column(at):
             return jnp.broadcast_to(
                 jnp.sum(
-                    jnp.where(lane_value == lane_wanted + float(at), picked, 0.0),
+                    jnp.where(lane_kind == at, picked, 0.0),
                     axis=1,
                     keepdims=True,
                 ),
@@ -512,8 +522,7 @@
             misfit[plane] = weight[...] * (observed[plane] - predicted[plane])
         last = iteration == ITERS - 1
         if last:
-            store = pltpu.make_async_copy(misfit, residual, store_sem)
-            store.start()
+            residual[...] = misfit[...]
 
         correlate(away, 0, iteration)
         swap = start_copy(
@@ -629,7 +638,6 @@
 
     square[0:members, :] = near_gain[...]
     final[...] = jnp.transpose(square[...])[:, 0:members]
-    store.wait()
     for copy in pending:
         copy.wait_send()
 
@@ -658,7 +666,7 @@
             jax.ShapeDtypeStruct((8, members, stations), f32),
         ),
         in_specs=[hbm] * 8,
-        out_specs=(vmem, hbm),
+        out_specs=(vmem, vmem),
         scratch_shapes=[
             pltpu.VMEM(positions.shape, f32),
             pltpu.VMEM(catalogue.shape, f32),
@@ -668,12 +676,13 @@
             pltpu.VMEM((8 * dirs, members), f32),
             pltpu.VMEM((8 * dirs, members), f32),
             dma((8,)),
-            dma,
             pltpu.VMEM((LANES, LANES), f32),
             pltpu.VMEM((8, LANES), f32),
             pltpu.VMEM((8, LANES), f32),
             pltpu.VMEM((chips, 8, LANES), f32),
             pltpu.VMEM((LANES, 2 * LANES), jnp.bfloat16),
+            pltpu.VMEM((dirs, slots, LANES), jnp.bfloat16),
+            pltpu.VMEM((dirs, slots, LANES), f32),
             dma((2,)),
             pltpu.VMEM((8, LANES), f32),
             pltpu.VMEM((groups, 8, LANES), f32),
@@ -712,17 +721,22 @@
             dma((ITERS,)),
         ],
         compiler_params=pltpu.CompilerParams(
-            collective_id=1, has_side_effects=True, vmem_limit_bytes=60 << 20
+            collective_id=1, has_side_effects=True, vmem_limit_bytes=24 << 20
         ),
     )(
-        positions,
-        catalogue,
-        cluster_ids,
-        counts,
-        flag_mask.reshape(members, stations),
-        thermal_noise.reshape(8, members, stations),
-        true_gains.reshape(8 * dirs, members),
-        start_gains.reshape(8 * dirs, members),
+        *(
+            pltpu.with_memory_space_constraint(array, pltpu.HBM)
+            for array in (
+                positions,
+                catalogue,
+                cluster_ids,
+                counts,
+                flag_mask.reshape(members, stations),
+                thermal_noise.reshape(8, members, stations),
+                true_gains.reshape(8 * dirs, members),
+                start_gains.reshape(8 * dirs, members),
+            )
+        )
     )
     return (final.reshape(true_gains.shape), residual.reshape(thermal_noise.shape))
 

time: 80.4 us -> 76.8 us (0.955)
  Pallas kernels: 77.4 us -> 74.8 us
  local copies, waits for them, and re-layouts: 2.17 us -> 1.29 us
    pallas_call x1, Pallas kernels: 77.4 us -> 74.8 us  [on_device(): pl.pallas_call(lambda *refs: kernel(sizes, *refs), name='calibrate', out_...]
    unnamed x4 -> x2, local copies, waits for them, and re-layouts: 2.17 us -> 1.29 us
where the time goes in v4:
time: 76.8 us; the launch traced here: 76.7 us
  Pallas kernels  74.8 us (97%)
  local copies, waits for them, and re-layouts  1.29 us (2%)
    pallas_call x1, Pallas kernels, on_device(): pl.pallas_call(lambda *refs: kernel(sizes, *refs), name='calibrate', out_...  74.8 us

profile of v4, /device:TPU:1, one launch (start us, length us, event | category | flops | bytes accessed | tf_op | source)
XLA Modules:
  0.0 76.7 jit_solution(12582058609757073853)
XLA Ops:
  0.6 74.8 %calibrate.1 = (f32[128,16]{1,0:T(8,128)S(1)}, f32[8,16,256]{2,1,0:T(8,128)S(1)}) custom-call(f32[3,16]{1,0:T(4,128)} %refs_0_.1, f32[7,32]{1,0:T(8,128)} %refs_1_.1, s32[16,64]{1,0:T(8,128)} %refs_2_.1, s32[16]{0:T(128)} %refs_3_.1, s32[16,256]{1,0:T(8,128)} %bitcast.13, f32[8,16,256]{2,1,0:T(8,128)} %bitcast.10, f32[128,16]{1,0:T(8,128)} %bitcast.11, ...), custom_call_target="tpu_custom_call" | custom-call | tf_op jit(solution)/shard_map/calibrate/pallas_call | solution.py:661
  75.4 0.6 copy.13
  76.0 0.7 copy.14

commit v5 on v4

--- a/solution.py
+++ b/solution.py
@@ -133,6 +133,7 @@
     place_rows,
     own_gains,
     every_gains,
+    gain_pair_sem,
     true_far,
     gain_far,
     near_true,
@@ -233,12 +234,20 @@
     square[:, 0:members] = start_gains[...]
     own_gains[:, LANES : 2 * LANES] = jnp.transpose(square[...])[0:members, :]
 
+    kept = pl.ds(pl.multiple_of(core * half, half), half)
+    away = pl.ds(pl.multiple_of((1 - core) * half, half), half)
+    every_gains[core, group] = own_gains[kept, :]
     gain_copies = [
-        start_copy(own_gains, every_gains.at[group], gain_send.at[i], gain_recv.at[i], peer)
+        start_copy(
+            every_gains.at[core, group],
+            every_gains.at[core, group],
+            gain_send.at[i],
+            gain_recv.at[i],
+            peer,
+        )
         for i, peer in enumerate(stn_peers)
     ]
     every_place[group] = own_place[...]
-    every_gains[group] = own_gains[...]
     near_true[...] = own_gains[:, 0:LANES]
     near_gain[...] = own_gains[:, LANES : 2 * LANES]
     for load in loads[4:]:
@@ -375,14 +384,25 @@
         coherent[direction] = result.reshape(8, members, stations)
         return carry
 
-    lax.fori_loop(0, dirs, model, 0, unroll=4)
-
+    lax.fori_loop(0, dirs // 2, model, 0, unroll=8)
     for copy in reversed(gain_copies):
         copy.wait_recv()
-    turned = jnp.transpose(every_gains[:, :, 0:LANES].reshape(stations, LANES))
-    true_far[...] = turned
-    turned = jnp.transpose(every_gains[:, :, LANES : 2 * LANES].reshape(stations, LANES))
-    gain_far[...] = turned
+    gain_hand = start_copy(
+        every_gains.at[core],
+        every_gains.at[core],
+        gain_pair_sem.at[0],
+        gain_pair_sem.at[1],
+        sibling,
+    )
+    lax.fori_loop(dirs // 2, dirs, model, 0, unroll=8)
+    gain_hand.wait_recv()
+
+    def far_rows(lanes):
+        tiles = [every_gains[at, other, :, lanes] for other in range(groups) for at in range(2)]
+        return jnp.transpose(jnp.concatenate(tiles, axis=0))
+
+    true_far[...] = far_rows(slice(0, LANES))
+    gain_far[...] = far_rows(slice(LANES, 2 * LANES))
 
     near_lane = lax.broadcasted_iota(jnp.int32, (members, LANES), 1)
     halves = [slice(at * LANES, (at + 1) * LANES) for at in range(stations // LANES)]
@@ -493,10 +513,10 @@
             return carry
 
         mine[iteration, at] = jnp.zeros((half, 2 * LANES), jnp.float32)
-        lax.fori_loop(0, dirs, body, 0, unroll=4)
+        lax.fori_loop(0, dirs, body, 0, unroll=8)
         mine[iteration, at, :, LANES : 2 * LANES] = normal[rows, :]
 
-    pending = [cat_swap] + cat_copies + place_copies + gain_copies
+    pending = [cat_swap, gain_hand] + cat_copies + place_copies + gain_copies
 
     def settle(copies):
         for copy in pending:
@@ -505,8 +525,6 @@
         for copy in reversed(copies):
             copy.wait_recv()
         pending.extend(copies)
-    kept = pl.ds(pl.multiple_of(core * half, half), half)
-    away = pl.ds(pl.multiple_of((1 - core) * half, half), half)
     normal[...] = jnp.zeros_like(normal)
 
     for iteration in range(ITERS):
@@ -688,7 +706,8 @@
             pltpu.VMEM((groups, 8, LANES), f32),
             pltpu.VMEM((8, stations), f32),
             pltpu.VMEM((members, 2 * LANES), f32),
-            pltpu.VMEM((groups, members, 2 * LANES), f32),
+            pltpu.VMEM((2, groups, half, 2 * LANES), f32),
+            dma((2,)),
             pltpu.VMEM((8 * dirs, stations), f32),
             pltpu.VMEM((8 * dirs, stations), f32),
             pltpu.VMEM((members, LANES), f32),

time: 76.8 us -> 75.1 us (0.978)
  Pallas kernels: 74.8 us -> 73.1 us
    pallas_call x1, Pallas kernels: 74.8 us -> 73.1 us  [on_device(): pl.pallas_call(lambda *refs: kernel(sizes, *refs), name='calibrate', out_...]
where the time goes in v5:
time: 75.1 us; the launch traced here: 75 us
  Pallas kernels  73.1 us (97%)
  local copies, waits for them, and re-layouts  1.29 us (2%)
    pallas_call x1, Pallas kernels, on_device(): pl.pallas_call(lambda *refs: kernel(sizes, *refs), name='calibrate', out_...  73.1 us

profile of v5, /device:TPU:1, one launch (start us, length us, event | category | flops | bytes accessed | tf_op | source)
XLA Modules:
  0.0 75.0 jit_solution(7287022648408955239)
XLA Ops:
  0.6 73.1 %calibrate.1 = (f32[128,16]{1,0:T(8,128)S(1)}, f32[8,16,256]{2,1,0:T(8,128)S(1)}) custom-call(f32[3,16]{1,0:T(4,128)} %refs_0_.1, f32[7,32]{1,0:T(8,128)} %refs_1_.1, s32[16,64]{1,0:T(8,128)} %refs_2_.1, s32[16]{0:T(128)} %refs_3_.1, s32[16,256]{1,0:T(8,128)} %bitcast.13, f32[8,16,256]{2,1,0:T(8,128)} %bitcast.10, f32[128,16]{1,0:T(8,128)} %bitcast.11, ...), custom_call_target="tpu_custom_call" | custom-call | tf_op jit(solution)/shard_map/calibrate/pallas_call | solution.py:679
  73.7 0.6 copy.13
  74.3 0.7 copy.14

commit v6 on v5

--- a/solution.py
+++ b/solution.py
@@ -500,7 +500,7 @@
                 for entry in range(4)
             ]
             found = mat_mul_adj(missed, turned_back)
-            collected = mine[iteration, at, :, 0:LANES]
+            collected = mine[iteration, at, 0:half, :]
             for entry in range(4):
                 for part in range(2):
                     value = sum(found[entry][part][:, lanes] for lanes in halves)
@@ -509,12 +509,16 @@
                         jnp.sum(value, axis=1, keepdims=True),
                         collected,
                     )
-            mine[iteration, at, :, 0:LANES] = collected
+            mine[iteration, at, 0:half, :] = collected
             return carry
 
-        mine[iteration, at] = jnp.zeros((half, 2 * LANES), jnp.float32)
+        mine[iteration, at, 0:half, :] = jnp.zeros((half, LANES), jnp.float32)
         lax.fori_loop(0, dirs, body, 0, unroll=8)
-        mine[iteration, at, :, LANES : 2 * LANES] = normal[rows, :]
+        powers = normal[rows, :]
+        beside = pltpu.roll(powers, LANES // 2, 1)
+        mine[iteration, at, half:, :] = jnp.where(
+            half_lane[0 : half // 2] < LANES // 2, powers[0 : half // 2], beside[half // 2 :]
+        )
 
     pending = [cat_swap, gain_hand] + cat_copies + place_copies + gain_copies
 
@@ -572,16 +576,18 @@
         def lanes_of(array, at):
             return pltpu.roll(array, LANES - at * dirs, 1) if at else array
 
+        powers = total[half:, :]
+        powers = jnp.concatenate([powers, pltpu.roll(powers, LANES // 2, 1)], axis=0)
         gains = near_gain[kept, :]
         current = [
             tuple(lanes_of(gains, part * 4 + entry) for part in range(2)) for entry in range(4)
         ]
         gathered = [
-            tuple(lanes_of(total[:, 0:LANES], part * 4 + entry) for part in range(2))
+            tuple(lanes_of(total[0:half, :], part * 4 + entry) for part in range(2))
             for entry in range(4)
         ]
         upper_diag, lower_diag, cross_real, cross_imag = (
-            lanes_of(total[:, LANES : 2 * LANES], at) for at in range(4)
+            lanes_of(powers, at) for at in range(4)
         )
         nothing = jnp.zeros_like(upper_diag)
         hermitian = [
@@ -719,9 +725,9 @@
             pltpu.VMEM((members, stations), f32),
             pltpu.VMEM((8, members, stations), f32),
             pltpu.VMEM((members, LANES), f32),
-            pltpu.VMEM((ITERS, half, 2 * LANES), f32),
-            pltpu.VMEM((ITERS, 2, half, 2 * LANES), f32),
-            pltpu.VMEM((ITERS, chips, half, 2 * LANES), f32),
+            pltpu.VMEM((ITERS, half + half // 2, LANES), f32),
+            pltpu.VMEM((ITERS, 2, half + half // 2, LANES), f32),
+            pltpu.VMEM((ITERS, chips, half + half // 2, LANES), f32),
             pltpu.VMEM((ITERS, half, LANES), f32),
             pltpu.VMEM((ITERS, 2, groups, half, LANES), f32),
             dma((chips - 1,)),

time: 75.1 us -> 74.4 us (level)
  no operation moved by 1% of the time
where the time goes in v6:
time: 74.4 us; the launch traced here: 74.3 us
  Pallas kernels  72.4 us (97%)
  local copies, waits for them, and re-layouts  1.29 us (2%)
    pallas_call x1, Pallas kernels, on_device(): pl.pallas_call(lambda *refs: kernel(sizes, *refs), name='calibrate', out_...  72.4 us

profile of v6, /device:TPU:1, one launch (start us, length us, event | category | flops | bytes accessed | tf_op | source)
XLA Modules:
  0.0 74.3 jit_solution(749940934778920927)
XLA Ops:
  0.6 72.4 %calibrate.1 = (f32[128,16]{1,0:T(8,128)S(1)}, f32[8,16,256]{2,1,0:T(8,128)S(1)}) custom-call(f32[3,16]{1,0:T(4,128)} %refs_0_.1, f32[7,32]{1,0:T(8,128)} %refs_1_.1, s32[16,64]{1,0:T(8,128)} %refs_2_.1, s32[16]{0:T(128)} %refs_3_.1, s32[16,256]{1,0:T(8,128)} %bitcast.13, f32[8,16,256]{2,1,0:T(8,128)} %bitcast.10, f32[128,16]{1,0:T(8,128)} %bitcast.11, ...), custom_call_target="tpu_custom_call" | custom-call | tf_op jit(solution)/shard_map/calibrate/pallas_call | solution.py:685
  73.0 0.6 copy.13
  73.7 0.7 copy.14

commit v7 on v6

--- a/solution.py
+++ b/solution.py
@@ -378,9 +378,10 @@
         def times(left, right):
             return jnp.dot(left, right, preferred_element_type=jnp.float32)
 
-        result = times(near_high, far_high) + (
-            times(near_low, far_high) + times(near_high, far_low)
-        )
+        result = times(
+            jnp.concatenate([near_high, near_low], axis=1),
+            jnp.concatenate([far_high, far_high], axis=0),
+        ) + times(near_high, far_low)
         coherent[direction] = result.reshape(8, members, stations)
         return carry
 

time: 74.4 us -> 74.3 us (level)
  no operation moved by 1% of the time
where the time goes in v7:
time: 74.3 us; the launch traced here: 74.2 us
  Pallas kernels  72.3 us (97%)
  local copies, waits for them, and re-layouts  1.29 us (2%)
    pallas_call x1, Pallas kernels, on_device(): pl.pallas_call(lambda *refs: kernel(sizes, *refs), name='calibrate', out_...  72.3 us

profile of v7, /device:TPU:1, one launch (start us, length us, event | category | flops | bytes accessed | tf_op | source)
XLA Modules:
  0.0 74.2 jit_solution(15098340277217188027)
XLA Ops:
  0.6 72.3 %calibrate.1 = (f32[128,16]{1,0:T(8,128)S(1)}, f32[8,16,256]{2,1,0:T(8,128)S(1)}) custom-call(f32[3,16]{1,0:T(4,128)} %refs_0_.1, f32[7,32]{1,0:T(8,128)} %refs_1_.1, s32[16,64]{1,0:T(8,128)} %refs_2_.1, s32[16]{0:T(128)} %refs_3_.1, s32[16,256]{1,0:T(8,128)} %bitcast.13, f32[8,16,256]{2,1,0:T(8,128)} %bitcast.10, f32[128,16]{1,0:T(8,128)} %bitcast.11, ...), custom_call_target="tpu_custom_call" | custom-call | tf_op jit(solution)/shard_map/calibrate/pallas_call | solution.py:686
  72.9 0.6 copy.13
  73.6 0.7 copy.14
